TPU v7x, 32 devices: a whole 2x2x4 slice. The times are simulated.
32 devices in a mesh: gx: 4 (over y, core), gy: 4 (over z), gz: 2 (over x).
Axes of the slice: x: 2, y: 2, z: 4, core: 2. Of those that a mesh axis runs over, the one named last changes fastest.
Arguments:
- w_minus: bfloat16 [4, 4, 2, 3, 512, 1024], P('gx', 'gy', 'gz'), may hold values from -0.25 to 0.25
- w_plus: bfloat16 [4, 4, 2, 3, 512, 1024], P('gx', 'gy', 'gz'), may hold values from -0.25 to 0.25
- interior: bfloat16 [4, 4, 2, 512, 512], P('gx', 'gy', 'gz')
- b_minus: bfloat16 [4, 4, 2, 3, 1024], P('gx', 'gy', 'gz'), may hold values from 2 to 4
- b_plus: bfloat16 [4, 4, 2, 3, 1024], P('gx', 'gy', 'gz'), may hold values from 2 to 4
- walls: int32 [4, 4, 2, 3], P('gx', 'gy', 'gz'), may hold values from 0 to 1, as said below
Outputs:
- assembled: bfloat16 [4, 4, 2, 3, 1024, 1024], P('gx', 'gy', 'gz')
Inputs may be any that keep to these rules, and one draw needn't show every extreme that they name: Every subdomain with the last index along axis a has walls 1 for axis a.
All inputs are finite; a program needn't handle non-finite values.
Results may differ from a plain program's by a relative error of at most 0.0039.
Values may be sent and summed in bfloat16 or wider, within the bound.
No kernel may reach another device: no remote copies, remote signals or barrier semaphores. Data moves between devices by JAX's collectives and lax.ppermute only.
A program may use at most 128 MiB of HBM per device.

v0:
```python
import functools

import jax
import jax.numpy as jnp
from jax import lax
from jax.experimental import pallas as pl
from jax.experimental.pallas import tpu as pltpu
from jax.sharding import PartitionSpec as P

FSIDE = 32
TILE = 128
STRIP = 256
BF16 = jnp.bfloat16
F32 = jnp.float32
AXES = ("gx", "gy", "gz")


def passed_along(array, axis):
    peers = lax.axis_size(axis)
    return lax.ppermute(array, axis, [(i + 1, i) for i in range(peers - 1)])


def in_vmem(array):
    return pltpu.with_memory_space_constraint(array, pltpu.VMEM)


def params(limit_mib):
    return pltpu.CompilerParams(vmem_limit_bytes=limit_mib << 20)


def spec(space):
    return pl.BlockSpec(memory_space=space)


def starts_of(cols):
    return [sum(cols[:i]) for i in range(len(cols))]


def link_tile(offset):
    p = lax.broadcasted_iota(jnp.int32, (TILE, TILE), 0)
    q = lax.broadcasted_iota(jnp.int32, (TILE, TILE), 1) + offset * TILE
    v = lax.rem(p, FSIDE)
    apart = q - p
    near = (jnp.abs(apart) == FSIDE) | ((apart == 1) & (v != FSIDE - 1)) | ((apart == -1) & (v != 0))
    return near.astype(F32)


def eye_tile():
    p = lax.broadcasted_iota(jnp.int32, (TILE, TILE), 0)
    q = lax.broadcasted_iota(jnp.int32, (TILE, TILE), 1)
    return p == q


def axis_of(turn):
    odd = lax.rem(lax.axis_index("gx"), 2)
    return jnp.where(odd == turn, 2, 1)


def pack_kernel(layout, rank, w_ref, a_ref, b_ref, *refs):
    outs, b_v, sems = refs[:-2], refs[-2], refs[-1]
    width = b_v.shape[1]
    axis_by_turn = [axis_of(turn) for turn in TURNS]
    copies = [pltpu.make_async_copy(b_ref, b_v, sems.at[0])]
    for n, ((turn, start, cols, with_b, with_a), out) in enumerate(zip(layout, outs)):
        axis_id = 0 if turn is None else axis_by_turn[turn]
        copies.append(
            pltpu.make_async_copy(
                w_ref.at[axis_id, :, pl.ds(start, cols)], out.at[pl.ds(0, rank), pl.ds(0, cols)], sems.at[n + 1]
            )
        )
        if with_a:
            copies.append(
                pltpu.make_async_copy(a_ref, out.at[pl.ds(0, rank), pl.ds(cols, rank)], sems.at[len(layout) + 1])
            )
    for copy in copies:
        copy.start()
    copies[0].wait()
    for (turn, start, cols, with_b, with_a), out in zip(layout, outs):
        if with_b:
            diag = b_v[0:1, :]
            if turn is not None:
                diag = jnp.where(axis_by_turn[turn] == 1, b_v[1:2, :], b_v[2:3, :])
            for i in range(0, width, cols):
                n = min(cols, width - i)
                out[rank + i // cols : rank + i // cols + 1, 0:n] = diag[:, i : i + n]
    for copy in copies[1:]:
        copy.wait()


def pack(w, a, b, layout):
    rank = w.shape[1]
    shapes = [(rank + 8 * with_b, cols + rank * with_a) for _, _, cols, with_b, with_a in layout]
    return pl.pallas_call(
        functools.partial(pack_kernel, layout, rank),
        out_shape=[pltpu.VMEM(s, BF16) for s in shapes],
        in_specs=[spec(pl.ANY)] * 3,
        out_specs=[spec(pltpu.VMEM)] * len(shapes),
        scratch_shapes=[pltpu.VMEM(b.shape, BF16), pltpu.SemaphoreType.DMA((len(shapes) + 2,))],
        compiler_params=params(8),
        name="pack",
    )(w, a, b)


def own_kernel(order, walls_hbm, a_ref, w_ref, b_hbm, base_ref, gate_ref, walls_ref, b_ref, a_v, w_v, mapped_v, sems):
    width = w_v.shape[2]
    a_copy = pltpu.make_async_copy(a_ref, a_v, sems.at[len(order)])
    a_copy.start()
    small = [
        pltpu.make_async_copy(walls_hbm, walls_ref, sems.at[len(order) + 1]),
        pltpu.make_async_copy(b_hbm, b_ref, sems.at[len(order) + 2]),
    ]
    for copy in small:
        copy.start()
    copies = []
    for n, axis_id in enumerate(order):
        copy = pltpu.make_async_copy(w_ref.at[axis_id], w_v.at[n], sems.at[n])
        copy.start()
        copies.append(copy)
    links = {offset: link_tile(offset) for offset in (-1, 0, 1)}
    eye = eye_tile()
    for copy in small:
        copy.wait()
    a_copy.wait()
    for n, axis_id in enumerate(order):
        copies[n].wait()
        opened = (walls_ref[axis_id] == 0).astype(F32)
        gate_ref[axis_id] = jnp.full((8, TILE), opened, F32)
        weight = 0.25 + 0.25 * opened
        mapped_v[...] = jnp.dot(a_v[...], w_v[n], preferred_element_type=F32).astype(BF16)
        for r in range(0, width, STRIP):
            base_ref[axis_id, r : r + STRIP, :] = -lax.dot_general(
                w_v[n, :, r : r + STRIP], mapped_v[...], (((0,), (0,)), ((), ())), preferred_element_type=F32
            )
        tiles = width // TILE
        for t in range(tiles):
            rows = pl.ds(t * TILE, TILE)
            for offset in (-1, 0, 1):
                if not 0 <= t + offset < tiles:
                    continue
                cols = pl.ds((t + offset) * TILE, TILE)
                add = -weight * links[offset]
                if offset == 0:
                    diag = b_ref[axis_id : axis_id + 1, t * TILE : (t + 1) * TILE].astype(F32)
                    add = add + jnp.where(eye, diag, 0.0)
                base_ref[axis_id, rows, cols] = base_ref[axis_id, rows, cols] + add


def own(walls, a, w, b, order):
    axes, rank, width = w.shape
    return pl.pallas_call(
        functools.partial(own_kernel, order),
        out_shape=[pltpu.VMEM((axes, width, width), F32), pltpu.VMEM((axes, 8, TILE), F32)],
        in_specs=[spec(pl.ANY)] * 4,
        out_specs=[spec(pltpu.VMEM)] * 2,
        scratch_shapes=[
            pltpu.SMEM(walls.shape, jnp.int32),
            pltpu.VMEM(b.shape, BF16),
            pltpu.VMEM((rank, rank), BF16),
            pltpu.VMEM((len(order), rank, width), BF16),
            pltpu.VMEM((rank, width), BF16),
            pltpu.SemaphoreType.DMA((len(order) + 3,)),
        ],
        compiler_params=params(24),
        cost_estimate=pl.CostEstimate(
            flops=2 * axes * rank * width * (rank + width), bytes_accessed=6 * axes * width * width, transcendentals=0
        ),
        name="own",
    )(walls, a, w, b)


def finish_kernel(turn, rank, cols, news, first, *refs):
    refs = list(refs)
    k = len(cols) - 1
    begin = starts_of(cols)
    s, c = begin[k], cols[k]

    def take(count):
        taken = refs[:count]
        del refs[:count]
        return taken

    gate_ref, base_ref, inverse, with_b = take(4)
    newest, turned, mapped = take(news), take(k), take(k)
    if not first:
        take(1)
    out_ref, fresh, turn_v, stage_col, stage_row, sems = refs
    copies = []

    def send(source, *where):
        copy = pltpu.make_async_copy(source, out_ref.at[where], sems.at[len(copies)])
        copy.start()
        copies.append(copy)

    axis_id = 0 if turn is None else axis_of(turn)
    opened = gate_ref[axis_id, 0:1, 0:1] > 0.5
    new = newest[0][0:rank, 0:c]
    if news > 1:
        new = jnp.concatenate([piece[0:rank, :] for piece in newest], axis=1)
    image = jnp.dot(inverse[0:rank, inverse.shape[1] - rank :], new, preferred_element_type=F32).astype(BF16)
    fresh[...] = jnp.where(opened, image, jnp.zeros_like(image))
    turn_v[...] = new.T
    if k:
        for j in range(k):
            at = slice(begin[j], begin[j] + cols[j])
            gram = jnp.dot(turn_v[...], mapped[j][...], preferred_element_type=F32)
            stage_row[:, at] = (base_ref[axis_id, s : s + c, at] - gram).astype(BF16)
        send(stage_row, axis_id, pl.ds(s, c), pl.ds(0, s))
    b_cols = with_b.shape[1] - (rank if turn is None else 0)
    for j in range(k + 1):
        left = turn_v if j == k else turned[j]
        for r in range(0, cols[j], STRIP):
            e = min(r + STRIP, cols[j])
            gram = jnp.dot(left[r:e, :], fresh[...], preferred_element_type=F32)
            total = base_ref[axis_id, begin[j] + r : begin[j] + e, s : s + c] - gram
            if j == k:
                p = lax.broadcasted_iota(jnp.int32, (e - r, c), 0) + r
                q = lax.broadcasted_iota(jnp.int32, (e - r, c), 1)
                diag = []
                for at in range(s, s + c, TILE):
                    i, start = divmod(at, b_cols)
                    diag.append(with_b[rank + i : rank + i + 1, start : start + TILE].astype(F32))
                diag = jnp.concatenate(diag, axis=1)
                total = total + jnp.where((p == q) & opened, diag, 0.0)
            rows = pl.ds(begin[j] + r, e - r)
            stage_col[rows, :] = total.astype(BF16)
            send(stage_col.at[rows], axis_id, rows, pl.ds(s, c))
    for copy in copies:
        copy.wait()


def finish(gate, base, inverse, with_b, newest, turned, mapped, out, turn, rank, cols, keep):
    axes, width, _ = base.shape
    k = len(cols) - 1
    s, c = starts_of(cols)[k], cols[k]
    first = out is None
    operands = [gate, base, inverse, with_b, *newest, *turned, *mapped]
    specs = [spec(pltpu.VMEM)] * len(operands)
    aliases = {}
    if not first:
        aliases = {len(operands): 0}
        operands.append(out)
        specs.append(spec(pl.ANY))
    kept = [pltpu.VMEM((rank, c), BF16), pltpu.VMEM((c, rank), BF16)]
    scratch = [
        pltpu.VMEM((s + c, c), BF16),
        pltpu.VMEM((c, max(s, TILE)), BF16),
        pltpu.SemaphoreType.DMA((1 + sum(-(-n // STRIP) for n in cols),)),
    ]
    shapes = [jax.ShapeDtypeStruct((axes, width, width), BF16)] + (kept if keep else [])
    return pl.pallas_call(
        functools.partial(finish_kernel, turn, rank, cols, len(newest), first),
        out_shape=shapes,
        in_specs=specs,
        out_specs=[spec(pl.ANY)] + [spec(pltpu.VMEM)] * (len(shapes) - 1),
        scratch_shapes=scratch if keep else kept + scratch,
        input_output_aliases=aliases,
        compiler_params=params(16),
        cost_estimate=pl.CostEstimate(
            flops=2 * rank * c * (rank + 2 * s + c), bytes_accessed=4 * width * c, transcendentals=0
        ),
    )(*operands)


def sends(array, turn):
    if turn is None:
        return passed_along(array, AXES[0])
    nx, ny, nz = (lax.axis_size(axis) for axis in AXES)
    pairs = []
    for i in range(nx):
        for j in range(ny):
            for k in range(nz):
                low = (i * ny + j) * nz + k
                if i % 2 == turn and k + 1 < nz:
                    pairs.append((low + 1, low))
                if i % 2 != turn and j + 1 < ny:
                    pairs.append((low + nz, low))
    return lax.ppermute(array, AXES, pairs)


def in_hbm(array):
    return pltpu.with_memory_space_constraint(array, pltpu.HBM)


TURNS = (0, 1)


def assemble(w_minus, w_plus, interior, b_minus, b_plus, walls):
    _, rank, width = w_plus.shape[3:]
    inverse = interior[0, 0, 0]
    w_minus, w_plus = w_minus[0, 0, 0], w_plus[0, 0, 0]
    b_minus, b_plus, walls = b_minus[0, 0, 0], b_plus[0, 0, 0], walls[0, 0, 0]
    most = width * 3 // 8
    cols = (width // 2, width // 4, width // 4)
    begin = starts_of(cols)

    far = [in_vmem(sends(inverse, turn)) for turn in TURNS]
    layout = [
        ("whole", None, 0, width, True, True),
        ("early", 0, 0, most, False, False),
        ("late", 0, most, width - most, True, False),
    ]
    layout += [(f"piece{k}", 1, begin[k], cols[k], k == 0, False) for k in range(len(cols))]
    packed = pack(in_hbm(w_minus), in_hbm(inverse), in_hbm(b_minus), [entry[1:] for entry in layout])
    whole, early, late, *pieces = [in_vmem(sends(p, entry[1])) for p, entry in zip(packed, layout)]
    base, gate = own(in_hbm(walls), in_hbm(inverse), in_hbm(w_plus), in_hbm(b_plus), (2, 1, 0))
    base, gate = in_vmem(base), in_vmem(gate)

    (out,) = finish(gate, base, whole, whole, [whole], [], [], None, None, rank, (width,), False)
    (out,) = finish(gate, base, far[0], late, [early, late], [], [], out, 0, rank, (width,), False)
    turned, mapped = [], []
    for k in range(len(cols)):
        out, *kept = finish(
            gate, base, far[1], pieces[0], pieces[k : k + 1], turned, mapped, out, 1, rank, cols[: k + 1],
            k + 1 < len(cols),
        )
        if kept:
            mapped = mapped + [in_vmem(kept[0])]
            turned = turned + [in_vmem(kept[1])]
    return out[None, None, None]


def solution(mesh):
    in_specs = (
        P("gx", "gy", "gz", None, None, None),
        P("gx", "gy", "gz", None, None, None),
        P("gx", "gy", "gz", None, None),
        P("gx", "gy", "gz", None, None),
        P("gx", "gy", "gz", None, None),
        P("gx", "gy", "gz", None),
    )
    out_specs = P("gx", "gy", "gz", None, None, None)
    return jax.shard_map(assemble, mesh=mesh, in_specs=in_specs, out_specs=out_specs, check_vma=False)
```

profile of v0, /device:TPU:1, one launch (start us, length us, event | category | flops | bytes accessed | tf_op | source)
XLA Modules:
  0.0 47.5 jit_solution(6090811137560975378)
XLA Ops:
  0.0 2.1 %pack.1 = (bf16[520,1536]{1,0:T(8,128)(2,1)S(1)}, bf16[512,384]{1,0:T(8,128)(2,1)S(1)}, bf16[520,640]{1,0:T(8,128)(2,1)S(1)}, bf16[520,512]{1,0:T(8,128)(2,1)S(1...) custom-call(bf16[3,512,1024]{2,1,0:T(8,128)(2,1)} %bitcast.7, bf16[512,512]{1,0:T(8,128)(2,1)} %bitcast.8, ...), custom_call_target="tpu_custom_call" | custom-call | tf_op jit(solution)/shard_map/pack/pallas_call | solution.py:93
  2.1 1.9 %collective-permute-start.6 = (bf16[520,1536]{1,0:T(8,128)(2,1)S(1)}, bf16[520,1536]{1,0:T(8,128)(2,1)S(1)}, u32[]{:S(2)}, u32[]{:S(2)}) collective-permute-start(bf16[520,1536]{1,0:T(8,128)(2,1)S(1)} %get-tuple-element.25), channel_id=1, source_target_pairs={{8,0},{16,8},{24,16},{9,1},{17,9},{25,17},{10,2},{18,10},{26,18},{... | collective-permute-start | bytes 4792328 | tf_op jit(solution)/shard_map/ppermute | solution.py:20
  4.0 1.3 %collective-permute-start.5 = (bf16[512,384]{1,0:T(8,128)(2,1)S(1)}, bf16[512,384]{1,0:T(8,128)(2,1)S(1)}, u32[]{:S(2)}, u32[]{:S(2)}) collective-permute-start(bf16[512,384]{1,0:T(8,128)(2,1)S(1)} %get-tuple-element.24), channel_id=1, source_target_pairs={{1,0},{3,2},{5,4},{7,6},{10,8},{11,9},{12,10},{13,11},{14,12},{15,... | collective-permute-start | bytes 1179656 | tf_op jit(solution)/shard_map/ppermute | solution.py:277
  5.3 1.3 %collective-permute-start.3 = (bf16[512,512]{1,0:T(8,128)(2,1)}, bf16[512,512]{1,0:T(8,128)(2,1)S(1)}, u32[]{:S(2)}, u32[]{:S(2)}) collective-permute-start(bf16[512,512]{1,0:T(8,128)(2,1)} %bitcast.9), channel_id=1, source_target_pairs={{1,0},{3,2},{5,4},{7,6},{10,8},{11,9},{12,10},{13,11},{14,12},{15,... | collective-permute-start | bytes 1572872 | tf_op jit(solution)/shard_map/ppermute | solution.py:277
  6.6 1.3 %collective-permute-start.4 = (bf16[520,640]{1,0:T(8,128)(2,1)S(1)}, bf16[520,640]{1,0:T(8,128)(2,1)S(1)}, u32[]{:S(2)}, u32[]{:S(2)}) collective-permute-start(bf16[520,640]{1,0:T(8,128)(2,1)S(1)} %get-tuple-element.23), channel_id=1, source_target_pairs={{1,0},{3,2},{5,4},{7,6},{10,8},{11,9},{12,10},{13,11},{14,12},{15,... | collective-permute-start | bytes 1996808 | tf_op jit(solution)/shard_map/ppermute | solution.py:277
  7.9 1.3 %collective-permute-start = (bf16[512,512]{1,0:T(8,128)(2,1)}, bf16[512,512]{1,0:T(8,128)(2,1)S(1)}, u32[]{:S(2)}, u32[]{:S(2)}) collective-permute-start(bf16[512,512]{1,0:T(8,128)(2,1)} %bitcast.10), channel_id=1, source_target_pairs={{2,0},{3,1},{4,2},{5,3},{6,4},{7,5},{9,8},{11,10},{13,12},{15,14},... | collective-permute-start | bytes 1572872 | tf_op jit(solution)/shard_map/ppermute | solution.py:277
  9.2 5.5 %collective-permute-done.5.refs_4_ = bf16[512,384]{1,0:T(8,128)(2,1)S(1)} collective-permute-done((bf16[512,384]{1,0:T(8,128)(2,1)S(1)}, bf16[512,384]{1,0:T(8,128)(2,1)S(1)}, u32[]{:S(2)}, u32[]{:S(2)}) %collective-permute-start.5) | collective-permute-done | bytes 393248 | tf_op jit(solution)/shard_map/ppermute | solution.py:277
  14.7 1.3 %collective-permute-start.1 = (bf16[520,512]{1,0:T(8,128)(2,1)S(1)}, bf16[520,512]{1,0:T(8,128)(2,1)S(1)}, u32[]{:S(2)}, u32[]{:S(2)}) collective-permute-start(bf16[520,512]{1,0:T(8,128)(2,1)S(1)} %get-tuple-element.21), channel_id=1, source_target_pairs={{2,0},{3,1},{4,2},{5,3},{6,4},{7,5},{9,8},{11,10},{13,12},{15,14},... | collective-permute-start | bytes 1597448 | tf_op jit(solution)/shard_map/ppermute | solution.py:277
  16.0 6.9 %own.1 = (f32[3,1024,1024]{2,1,0:T(8,128)S(1)}, f32[3,8,128]{2,1,0:T(8,128)S(1)}) custom-call(s32[3]{0:T(128)} %bitcast.15, bf16[512,512]{1,0:T(8,128)(2,1)} %bitcast.11, bf16[3,512,1024]{2,1,0:T(8,128)(2,1)} %bitcast.13, bf16[3,1024]{1,0:T(4,128)(2,1)} %bitcast.14), custom_call_target="tpu_custom_call" | custom-call | flops 4831838208 | bytes 18874368 | tf_op jit(solution)/shard_map/own/pallas_call | solution.py:150
  22.9 3.1 %collective-permute-done.3.refs_2_ = bf16[512,512]{1,0:T(8,128)(2,1)S(1)} collective-permute-done((bf16[512,512]{1,0:T(8,128)(2,1)}, bf16[512,512]{1,0:T(8,128)(2,1)S(1)}, u32[]{:S(2)}, u32[]{:S(2)}) %collective-permute-start.3) | collective-permute-done | bytes 524320 | tf_op jit(solution)/shard_map/ppermute | solution.py:277
  25.9 1.3 %collective-permute-start.7 = (bf16[512,256]{1,0:T(8,128)(2,1)S(1)}, bf16[512,256]{1,0:T(8,128)(2,1)S(1)}, u32[]{:S(2)}, u32[]{:S(2)}) collective-permute-start(bf16[512,256]{1,0:T(8,128)(2,1)S(1)} %get-tuple-element.27), channel_id=1, source_target_pairs={{2,0},{3,1},{4,2},{5,3},{6,4},{7,5},{9,8},{11,10},{13,12},{15,14},... | collective-permute-start | bytes 786440 | tf_op jit(solution)/shard_map/ppermute | solution.py:277
  27.2 0.0 collective-permute-done.6.refs_2_.refs_3_.refs_4_
  27.2 1.3 %collective-permute-start.2 = (bf16[512,256]{1,0:T(8,128)(2,1)S(1)}, bf16[512,256]{1,0:T(8,128)(2,1)S(1)}, u32[]{:S(2)}, u32[]{:S(2)}) collective-permute-start(bf16[512,256]{1,0:T(8,128)(2,1)S(1)} %get-tuple-element.22), channel_id=1, source_target_pairs={{2,0},{3,1},{4,2},{5,3},{6,4},{7,5},{9,8},{11,10},{13,12},{15,14},... | collective-permute-start | bytes 786440 | tf_op jit(solution)/shard_map/ppermute | solution.py:277
  28.5 2.7 %shard_map.64.refs_6_ = bf16[3,1024,1024]{2,1,0:T(8,128)(2,1)} custom-call(f32[3,8,128]{2,1,0:T(8,128)S(1)} %get-tuple-element.19.refs_0_, f32[3,1024,1024]{2,1,0:T(8,128)S(1)} %get-tuple-element.20.refs_1_, bf16[520,1536]{1,0:T(8,128)(2,1)S(1)} %collective-permute-done.6.refs_2_.refs_3_.refs_4_, ...), custom_call_target="tpu_custom_call" | custom-call | flops 1610612736 | bytes 4194304 | tf_op jit(solution)/shard_map/pallas_call | solution.py:250
  31.2 8.9 %collective-permute-done.4.refs_3_.refs_5_ = bf16[520,640]{1,0:T(8,128)(2,1)S(1)} collective-permute-done((bf16[520,640]{1,0:T(8,128)(2,1)S(1)}, bf16[520,640]{1,0:T(8,128)(2,1)S(1)}, u32[]{:S(2)}, u32[]{:S(2)}) %collective-permute-start.4) | collective-permute-done | bytes 665632 | tf_op jit(solution)/shard_map/ppermute | solution.py:277
  40.2 2.7 %shard_map.65.refs_5_ = bf16[3,1024,1024]{2,1,0:T(8,128)(2,1)} custom-call(f32[3,8,128]{2,1,0:T(8,128)S(1)} %get-tuple-element.19.refs_0_, f32[3,1024,1024]{2,1,0:T(8,128)S(1)} %get-tuple-element.20.refs_1_, bf16[512,512]{1,0:T(8,128)(2,1)S(1)} %collective-permute-done.3.refs_2_, ...), custom_call_target="tpu_custom_call", output_to_operand_aliasing={{}: (6, {})} | custom-call | flops 1610612736 | bytes 4194304 | tf_op jit(solution)/shard_map/pallas_call | solution.py:250
  42.9 0.0 collective-permute-done.refs_2_
  42.9 0.0 collective-permute-done.1.refs_3_.refs_4_
  42.9 1.5 %shard_map.66 = (bf16[3,1024,1024]{2,1,0:T(8,128)(2,1)}, bf16[512,512]{1,0:T(8,128)(2,1)S(1)}, bf16[512,512]{1,0:T(8,128)(2,1)S(1)}) custom-call(f32[3,8,128]{2,1,0:T(8,128)S(1)} %get-tuple-element.19.refs_0_, f32[3,1024,1024]{2,1,0:T(8,128)S(1)} %get-tuple-element.20.refs_1_, ...), custom_call_target="tpu_custom_call", output_to_operand_aliasing={{0}: (5, {})} | custom-call | flops 536870912 | bytes 2097152 | tf_op jit(solution)/shard_map/pallas_call | solution.py:250
  44.5 0.0 collective-permute-done.7.refs_4_
  44.5 1.4 %shard_map.67 = (bf16[3,1024,1024]{2,1,0:T(8,128)(2,1)}, bf16[512,256]{1,0:T(8,128)(2,1)S(1)}, bf16[256,512]{1,0:T(8,128)(2,1)S(1)}) custom-call(f32[3,8,128]{2,1,0:T(8,128)S(1)} %get-tuple-element.19.refs_0_, f32[3,1024,1024]{2,1,0:T(8,128)S(1)} %get-tuple-element.20.refs_1_, ...), custom_call_target="tpu_custom_call", output_to_operand_aliasing={{0}: (7, {})} | custom-call | flops 469762048 | bytes 1048576 | tf_op jit(solution)/shard_map/pallas_call | solution.py:250
  45.9 0.0 collective-permute-done.2.refs_4_
  45.9 1.6 %shard_map.68 = bf16[3,1024,1024]{2,1,0:T(8,128)(2,1)} custom-call(f32[3,8,128]{2,1,0:T(8,128)S(1)} %get-tuple-element.19.refs_0_, f32[3,1024,1024]{2,1,0:T(8,128)S(1)} %get-tuple-element.20.refs_1_, bf16[512,512]{1,0:T(8,128)(2,1)S(1)} %collective-permute-done.refs_2_, ...), custom_call_target="tpu_custom_call", output_to_operand_aliasing={{}: (9, {})} | custom-call | flops 603979776 | bytes 1048576 | tf_op jit(solution)/shard_map/pallas_call | solution.py:250
Async XLA Ops:
  2.1 25.1 %collective-permute-start.6 = (bf16[520,1536]{1,0:T(8,128)(2,1)S(1)}, bf16[520,1536]{1,0:T(8,128)(2,1)S(1)}, u32[]{:S(2)}, u32[]{:S(2)}) collective-permute-start(bf16[520,1536]{1,0:T(8,128)(2,1)S(1)} %get-tuple-element.25), channel_id=1, source_target_pairs={{8,0},{16,8},{24,16},{9,1},{17,9},{25,17},{10,2},{18,10},{26,18},{... | collective-permute-start | bytes 4792328 | tf_op jit(solution)/shard_map/ppermute | solution.py:20
  4.0 10.7 %collective-permute-start.5 = (bf16[512,384]{1,0:T(8,128)(2,1)S(1)}, bf16[512,384]{1,0:T(8,128)(2,1)S(1)}, u32[]{:S(2)}, u32[]{:S(2)}) collective-permute-start(bf16[512,384]{1,0:T(8,128)(2,1)S(1)} %get-tuple-element.24), channel_id=1, source_target_pairs={{1,0},{3,2},{5,4},{7,6},{10,8},{11,9},{12,10},{13,11},{14,12},{15,... | collective-permute-start | bytes 1179656 | tf_op jit(solution)/shard_map/ppermute | solution.py:277
  5.3 20.6 %collective-permute-start.3 = (bf16[512,512]{1,0:T(8,128)(2,1)}, bf16[512,512]{1,0:T(8,128)(2,1)S(1)}, u32[]{:S(2)}, u32[]{:S(2)}) collective-permute-start(bf16[512,512]{1,0:T(8,128)(2,1)} %bitcast.9), channel_id=1, source_target_pairs={{1,0},{3,2},{5,4},{7,6},{10,8},{11,9},{12,10},{13,11},{14,12},{15,... | collective-permute-start | bytes 1572872 | tf_op jit(solution)/shard_map/ppermute | solution.py:277
  6.6 33.6 %collective-permute-start.4 = (bf16[520,640]{1,0:T(8,128)(2,1)S(1)}, bf16[520,640]{1,0:T(8,128)(2,1)S(1)}, u32[]{:S(2)}, u32[]{:S(2)}) collective-permute-start(bf16[520,640]{1,0:T(8,128)(2,1)S(1)} %get-tuple-element.23), channel_id=1, source_target_pairs={{1,0},{3,2},{5,4},{7,6},{10,8},{11,9},{12,10},{13,11},{14,12},{15,... | collective-permute-start | bytes 1996808 | tf_op jit(solution)/shard_map/ppermute | solution.py:277
  7.9 35.0 %collective-permute-start = (bf16[512,512]{1,0:T(8,128)(2,1)}, bf16[512,512]{1,0:T(8,128)(2,1)S(1)}, u32[]{:S(2)}, u32[]{:S(2)}) collective-permute-start(bf16[512,512]{1,0:T(8,128)(2,1)} %bitcast.10), channel_id=1, source_target_pairs={{2,0},{3,1},{4,2},{5,3},{6,4},{7,5},{9,8},{11,10},{13,12},{15,14},... | collective-permute-start | bytes 1572872 | tf_op jit(solution)/shard_map/ppermute | solution.py:277
  14.7 28.3 %collective-permute-start.1 = (bf16[520,512]{1,0:T(8,128)(2,1)S(1)}, bf16[520,512]{1,0:T(8,128)(2,1)S(1)}, u32[]{:S(2)}, u32[]{:S(2)}) collective-permute-start(bf16[520,512]{1,0:T(8,128)(2,1)S(1)} %get-tuple-element.21), channel_id=1, source_target_pairs={{2,0},{3,1},{4,2},{5,3},{6,4},{7,5},{9,8},{11,10},{13,12},{15,14},... | collective-permute-start | bytes 1597448 | tf_op jit(solution)/shard_map/ppermute | solution.py:277
  25.9 18.6 %collective-permute-start.7 = (bf16[512,256]{1,0:T(8,128)(2,1)S(1)}, bf16[512,256]{1,0:T(8,128)(2,1)S(1)}, u32[]{:S(2)}, u32[]{:S(2)}) collective-permute-start(bf16[512,256]{1,0:T(8,128)(2,1)S(1)} %get-tuple-element.27), channel_id=1, source_target_pairs={{2,0},{3,1},{4,2},{5,3},{6,4},{7,5},{9,8},{11,10},{13,12},{15,14},... | collective-permute-start | bytes 786440 | tf_op jit(solution)/shard_map/ppermute | solution.py:277
  27.2 18.7 %collective-permute-start.2 = (bf16[512,256]{1,0:T(8,128)(2,1)S(1)}, bf16[512,256]{1,0:T(8,128)(2,1)S(1)}, u32[]{:S(2)}, u32[]{:S(2)}) collective-permute-start(bf16[512,256]{1,0:T(8,128)(2,1)S(1)} %get-tuple-element.22), channel_id=1, source_target_pairs={{2,0},{3,1},{4,2},{5,3},{6,4},{7,5},{9,8},{11,10},{13,12},{15,14},... | collective-permute-start | bytes 786440 | tf_op jit(solution)/shard_map/ppermute | solution.py:277
where the time goes:
time: 47.8 us; the launch traced here: 47.5 us
  Pallas kernels  18.9 us (40%)
  waiting for transfers between devices  17.5 us (37%)
  starting transfers between devices  10.9 us (23%)
    ppermute x7, waiting for transfers between devices, sends(): return lax.ppermute(array, AXES, pairs)  17.5 us
    pallas_call x5, Pallas kernels, finish(): pl.pallas_call(functools.partial(finish_kernel, turn, rank, cols, len(new...  9.99 us
    ppermute x7, starting transfers between devices, sends(): return lax.ppermute(array, AXES, pairs)  9.02 us
    pallas_call x1, Pallas kernels, own(): pl.pallas_call(functools.partial(own_kernel, order), out_shape=[pltpu.VME...  6.88 us
    pallas_call x1, Pallas kernels, pack(): pl.pallas_call(functools.partial(pack_kernel, layout, rank), out_shape=[p...  2.07 us
    ppermute x1, starting transfers between devices, passed_along(): return lax.ppermute(array, axis, [(i + 1, i) for i in range(peers - 1)])  1.93 us
  transfers between devices with their start and end apart: 8, of which 3 were waited for; matrix products, arithmetic and copies ran while one was open for 0% of the time, Pallas kernels for 32%

commit v1 on v0

--- a/solution.py
+++ b/solution.py
@@ -289,15 +289,15 @@
     inverse = interior[0, 0, 0]
     w_minus, w_plus = w_minus[0, 0, 0], w_plus[0, 0, 0]
     b_minus, b_plus, walls = b_minus[0, 0, 0], b_plus[0, 0, 0], walls[0, 0, 0]
-    most = width * 3 // 8
-    cols = (width // 2, width // 4, width // 4)
+    most = width // 4
+    cols = (width * 3 // 8, width * 3 // 8, width // 4)
     begin = starts_of(cols)
 
     far = [in_vmem(sends(inverse, turn)) for turn in TURNS]
     layout = [
         ("whole", None, 0, width, True, True),
-        ("early", 0, 0, most, False, False),
-        ("late", 0, most, width - most, True, False),
+        ("early", 0, 0, most, True, False),
+        ("late", 0, most, width - most, False, False),
     ]
     layout += [(f"piece{k}", 1, begin[k], cols[k], k == 0, False) for k in range(len(cols))]
     packed = pack(in_hbm(w_minus), in_hbm(inverse), in_hbm(b_minus), [entry[1:] for entry in layout])
@@ -306,7 +306,7 @@
     base, gate = in_vmem(base), in_vmem(gate)
 
     (out,) = finish(gate, base, whole, whole, [whole], [], [], None, None, rank, (width,), False)
-    (out,) = finish(gate, base, far[0], late, [early, late], [], [], out, 0, rank, (width,), False)
+    (out,) = finish(gate, base, far[0], early, [early, late], [], [], out, 0, rank, (width,), False)
     turned, mapped = [], []
     for k in range(len(cols)):
         out, *kept = finish(

time: 47.8 us -> 47.8 us (level)
  the two profiles are of different devices: /device:TPU:1 before, /device:TPU:28 now
where the time goes in v1:
time: 47.8 us; the launch traced here: 47.5 us
  Pallas kernels  19.3 us (40%)
  starting transfers between devices  17.7 us (37%)
  waiting for transfers between devices  10.4 us (22%)
    ppermute x7, starting transfers between devices, sends(): return lax.ppermute(array, AXES, pairs)  15.7 us
    ppermute x7, waiting for transfers between devices, sends(): return lax.ppermute(array, AXES, pairs)  10.4 us
    pallas_call x5, Pallas kernels, finish(): pl.pallas_call(functools.partial(finish_kernel, turn, rank, cols, len(new...  10.3 us
    pallas_call x1, Pallas kernels, own(): pl.pallas_call(functools.partial(own_kernel, order), out_shape=[pltpu.VME...  6.88 us
    pallas_call x1, Pallas kernels, pack(): pl.pallas_call(functools.partial(pack_kernel, layout, rank), out_shape=[p...  2.07 us
    ppermute x1, starting transfers between devices, passed_along(): return lax.ppermute(array, axis, [(i + 1, i) for i in range(peers - 1)])  1.92 us
  transfers between devices with their start and end apart: 8, of which 1 were waited for; matrix products, arithmetic and copies ran while one was open for 0% of the time, Pallas kernels for 33%

profile of v1, /device:TPU:28, one launch (start us, length us, event | category | flops | bytes accessed | tf_op | source)
XLA Modules:
  0.0 47.5 jit_solution(13420818269601927827)
XLA Ops:
  0.0 2.1 %pack.1 = (bf16[520,1536]{1,0:T(8,128)(2,1)S(1)}, bf16[520,256]{1,0:T(8,128)(2,1)S(1)}, bf16[512,768]{1,0:T(8,128)(2,1)S(1)}, bf16[520,384]{1,0:T(8,128)(2,1)S(1...) custom-call(bf16[3,512,1024]{2,1,0:T(8,128)(2,1)} %bitcast.7, bf16[512,512]{1,0:T(8,128)(2,1)} %bitcast.8, ...), custom_call_target="tpu_custom_call" | custom-call | tf_op jit(solution)/shard_map/pack/pallas_call | solution.py:93
  2.1 1.9 %collective-permute-start.6 = (bf16[520,1536]{1,0:T(8,128)(2,1)S(1)}, bf16[520,1536]{1,0:T(8,128)(2,1)S(1)}, u32[]{:S(2)}, u32[]{:S(2)}) collective-permute-start(bf16[520,1536]{1,0:T(8,128)(2,1)S(1)} %get-tuple-element.25), channel_id=1, source_target_pairs={{8,0},{16,8},{24,16},{9,1},{17,9},{25,17},{10,2},{18,10},{26,18},{... | collective-permute-start | bytes 4792328 | tf_op jit(solution)/shard_map/ppermute | solution.py:20
  4.0 1.3 %collective-permute-start.3 = (bf16[512,512]{1,0:T(8,128)(2,1)}, bf16[512,512]{1,0:T(8,128)(2,1)S(1)}, u32[]{:S(2)}, u32[]{:S(2)}) collective-permute-start(bf16[512,512]{1,0:T(8,128)(2,1)} %bitcast.9), channel_id=1, source_target_pairs={{1,0},{3,2},{5,4},{7,6},{10,8},{11,9},{12,10},{13,11},{14,12},{15,... | collective-permute-start | bytes 1572872 | tf_op jit(solution)/shard_map/ppermute | solution.py:277
  5.3 1.3 %collective-permute-start.4 = (bf16[520,256]{1,0:T(8,128)(2,1)S(1)}, bf16[520,256]{1,0:T(8,128)(2,1)S(1)}, u32[]{:S(2)}, u32[]{:S(2)}) collective-permute-start(bf16[520,256]{1,0:T(8,128)(2,1)S(1)} %get-tuple-element.23), channel_id=1, source_target_pairs={{1,0},{3,2},{5,4},{7,6},{10,8},{11,9},{12,10},{13,11},{14,12},{15,... | collective-permute-start | bytes 798728 | tf_op jit(solution)/shard_map/ppermute | solution.py:277
  6.6 1.3 %collective-permute-start.5 = (bf16[512,768]{1,0:T(8,128)(2,1)S(1)}, bf16[512,768]{1,0:T(8,128)(2,1)S(1)}, u32[]{:S(2)}, u32[]{:S(2)}) collective-permute-start(bf16[512,768]{1,0:T(8,128)(2,1)S(1)} %get-tuple-element.24), channel_id=1, source_target_pairs={{1,0},{3,2},{5,4},{7,6},{10,8},{11,9},{12,10},{13,11},{14,12},{15,... | collective-permute-start | bytes 2359304 | tf_op jit(solution)/shard_map/ppermute | solution.py:277
  7.9 2.4 %collective-permute-start = (bf16[512,512]{1,0:T(8,128)(2,1)}, bf16[512,512]{1,0:T(8,128)(2,1)S(1)}, u32[]{:S(2)}, u32[]{:S(2)}) collective-permute-start(bf16[512,512]{1,0:T(8,128)(2,1)} %bitcast.10), channel_id=1, source_target_pairs={{2,0},{3,1},{4,2},{5,3},{6,4},{7,5},{9,8},{11,10},{13,12},{15,14},... | collective-permute-start | bytes 1572872 | tf_op jit(solution)/shard_map/ppermute | solution.py:277
  10.3 10.4 %collective-permute-done.4.refs_3_.refs_4_ = bf16[520,256]{1,0:T(8,128)(2,1)S(1)} collective-permute-done((bf16[520,256]{1,0:T(8,128)(2,1)S(1)}, bf16[520,256]{1,0:T(8,128)(2,1)S(1)}, u32[]{:S(2)}, u32[]{:S(2)}) %collective-permute-start.4) | collective-permute-done | bytes 266272 | tf_op jit(solution)/shard_map/ppermute | solution.py:277
  20.7 2.6 %collective-permute-start.1 = (bf16[520,384]{1,0:T(8,128)(2,1)S(1)}, bf16[520,384]{1,0:T(8,128)(2,1)S(1)}, u32[]{:S(2)}, u32[]{:S(2)}) collective-permute-start(bf16[520,384]{1,0:T(8,128)(2,1)S(1)} %get-tuple-element.21), channel_id=1, source_target_pairs={{2,0},{3,1},{4,2},{5,3},{6,4},{7,5},{9,8},{11,10},{13,12},{15,14},... | collective-permute-start | bytes 1198088 | tf_op jit(solution)/shard_map/ppermute | solution.py:277
  23.3 0.0 collective-permute-done.3.refs_2_
  23.3 2.5 %collective-permute-start.7 = (bf16[512,384]{1,0:T(8,128)(2,1)S(1)}, bf16[512,384]{1,0:T(8,128)(2,1)S(1)}, u32[]{:S(2)}, u32[]{:S(2)}) collective-permute-start(bf16[512,384]{1,0:T(8,128)(2,1)S(1)} %get-tuple-element.27), channel_id=1, source_target_pairs={{2,0},{3,1},{4,2},{5,3},{6,4},{7,5},{9,8},{11,10},{13,12},{15,14},... | collective-permute-start | bytes 1179656 | tf_op jit(solution)/shard_map/ppermute | solution.py:277
  25.8 6.9 %own.1 = (f32[3,1024,1024]{2,1,0:T(8,128)S(1)}, f32[3,8,128]{2,1,0:T(8,128)S(1)}) custom-call(s32[3]{0:T(128)} %bitcast.15, bf16[512,512]{1,0:T(8,128)(2,1)} %bitcast.11, bf16[3,512,1024]{2,1,0:T(8,128)(2,1)} %bitcast.13, bf16[3,1024]{1,0:T(4,128)(2,1)} %bitcast.14), custom_call_target="tpu_custom_call" | custom-call | flops 4831838208 | bytes 18874368 | tf_op jit(solution)/shard_map/own/pallas_call | solution.py:150
  32.7 0.0 collective-permute-done.6.refs_2_.refs_3_.refs_4_
  32.7 4.4 %collective-permute-start.2 = (bf16[512,256]{1,0:T(8,128)(2,1)S(1)}, bf16[512,256]{1,0:T(8,128)(2,1)S(1)}, u32[]{:S(2)}, u32[]{:S(2)}) collective-permute-start(bf16[512,256]{1,0:T(8,128)(2,1)S(1)} %get-tuple-element.22), channel_id=1, source_target_pairs={{2,0},{3,1},{4,2},{5,3},{6,4},{7,5},{9,8},{11,10},{13,12},{15,14},... | collective-permute-start | bytes 786440 | tf_op jit(solution)/shard_map/ppermute | solution.py:277
  37.1 2.7 %shard_map.64.refs_6_ = bf16[3,1024,1024]{2,1,0:T(8,128)(2,1)} custom-call(f32[3,8,128]{2,1,0:T(8,128)S(1)} %get-tuple-element.19.refs_0_, f32[3,1024,1024]{2,1,0:T(8,128)S(1)} %get-tuple-element.20.refs_1_, bf16[520,1536]{1,0:T(8,128)(2,1)S(1)} %collective-permute-done.6.refs_2_.refs_3_.refs_4_, ...), custom_call_target="tpu_custom_call" | custom-call | flops 1610612736 | bytes 4194304 | tf_op jit(solution)/shard_map/pallas_call | solution.py:250
  39.8 0.0 collective-permute-done.5.refs_5_
  39.8 2.7 %shard_map.65.refs_5_ = bf16[3,1024,1024]{2,1,0:T(8,128)(2,1)} custom-call(f32[3,8,128]{2,1,0:T(8,128)S(1)} %get-tuple-element.19.refs_0_, f32[3,1024,1024]{2,1,0:T(8,128)S(1)} %get-tuple-element.20.refs_1_, bf16[512,512]{1,0:T(8,128)(2,1)S(1)} %collective-permute-done.3.refs_2_, ...), custom_call_target="tpu_custom_call", output_to_operand_aliasing={{}: (6, {})} | custom-call | flops 1610612736 | bytes 4194304 | tf_op jit(solution)/shard_map/pallas_call | solution.py:250
  42.6 0.0 collective-permute-done.1.refs_3_.refs_4_
  42.6 0.0 collective-permute-done.refs_2_
  42.6 1.4 %shard_map.66 = (bf16[3,1024,1024]{2,1,0:T(8,128)(2,1)}, bf16[512,384]{1,0:T(8,128)(2,1)S(1)}, bf16[384,512]{1,0:T(8,128)(2,1)S(1)}) custom-call(f32[3,8,128]{2,1,0:T(8,128)S(1)} %get-tuple-element.19.refs_0_, f32[3,1024,1024]{2,1,0:T(8,128)S(1)} %get-tuple-element.20.refs_1_, ...), custom_call_target="tpu_custom_call", output_to_operand_aliasing={{0}: (5, {})} | custom-call | flops 352321536 | bytes 1572864 | tf_op jit(solution)/shard_map/pallas_call | solution.py:250
  44.0 0.0 collective-permute-done.7.refs_4_
  44.0 1.8 %shard_map.67 = (bf16[3,1024,1024]{2,1,0:T(8,128)(2,1)}, bf16[512,384]{1,0:T(8,128)(2,1)S(1)}, bf16[384,512]{1,0:T(8,128)(2,1)S(1)}) custom-call(f32[3,8,128]{2,1,0:T(8,128)S(1)} %get-tuple-element.19.refs_0_, f32[3,1024,1024]{2,1,0:T(8,128)S(1)} %get-tuple-element.20.refs_1_, ...), custom_call_target="tpu_custom_call", output_to_operand_aliasing={{0}: (7, {})} | custom-call | flops 654311424 | bytes 1572864 | tf_op jit(solution)/shard_map/pallas_call | solution.py:250
  45.8 0.0 collective-permute-done.2.refs_4_
  45.8 1.7 %shard_map.68 = bf16[3,1024,1024]{2,1,0:T(8,128)(2,1)} custom-call(f32[3,8,128]{2,1,0:T(8,128)S(1)} %get-tuple-element.19.refs_0_, f32[3,1024,1024]{2,1,0:T(8,128)S(1)} %get-tuple-element.20.refs_1_, bf16[512,512]{1,0:T(8,128)(2,1)S(1)} %collective-permute-done.refs_2_, ...), custom_call_target="tpu_custom_call", output_to_operand_aliasing={{}: (9, {})} | custom-call | flops 603979776 | bytes 1048576 | tf_op jit(solution)/shard_map/pallas_call | solution.py:250
Async XLA Ops:
  2.1 30.6 %collective-permute-start.6 = (bf16[520,1536]{1,0:T(8,128)(2,1)S(1)}, bf16[520,1536]{1,0:T(8,128)(2,1)S(1)}, u32[]{:S(2)}, u32[]{:S(2)}) collective-permute-start(bf16[520,1536]{1,0:T(8,128)(2,1)S(1)} %get-tuple-element.25), channel_id=1, source_target_pairs={{8,0},{16,8},{24,16},{9,1},{17,9},{25,17},{10,2},{18,10},{26,18},{... | collective-permute-start | bytes 4792328 | tf_op jit(solution)/shard_map/ppermute | solution.py:20
  4.0 19.3 %collective-permute-start.3 = (bf16[512,512]{1,0:T(8,128)(2,1)}, bf16[512,512]{1,0:T(8,128)(2,1)S(1)}, u32[]{:S(2)}, u32[]{:S(2)}) collective-permute-start(bf16[512,512]{1,0:T(8,128)(2,1)} %bitcast.9), channel_id=1, source_target_pairs={{1,0},{3,2},{5,4},{7,6},{10,8},{11,9},{12,10},{13,11},{14,12},{15,... | collective-permute-start | bytes 1572872 | tf_op jit(solution)/shard_map/ppermute | solution.py:277
  5.3 15.4 %collective-permute-start.4 = (bf16[520,256]{1,0:T(8,128)(2,1)S(1)}, bf16[520,256]{1,0:T(8,128)(2,1)S(1)}, u32[]{:S(2)}, u32[]{:S(2)}) collective-permute-start(bf16[520,256]{1,0:T(8,128)(2,1)S(1)} %get-tuple-element.23), channel_id=1, source_target_pairs={{1,0},{3,2},{5,4},{7,6},{10,8},{11,9},{12,10},{13,11},{14,12},{15,... | collective-permute-start | bytes 798728 | tf_op jit(solution)/shard_map/ppermute | solution.py:277
  6.6 33.2 %collective-permute-start.5 = (bf16[512,768]{1,0:T(8,128)(2,1)S(1)}, bf16[512,768]{1,0:T(8,128)(2,1)S(1)}, u32[]{:S(2)}, u32[]{:S(2)}) collective-permute-start(bf16[512,768]{1,0:T(8,128)(2,1)S(1)} %get-tuple-element.24), channel_id=1, source_target_pairs={{1,0},{3,2},{5,4},{7,6},{10,8},{11,9},{12,10},{13,11},{14,12},{15,... | collective-permute-start | bytes 2359304 | tf_op jit(solution)/shard_map/ppermute | solution.py:277
  7.9 34.7 %collective-permute-start = (bf16[512,512]{1,0:T(8,128)(2,1)}, bf16[512,512]{1,0:T(8,128)(2,1)S(1)}, u32[]{:S(2)}, u32[]{:S(2)}) collective-permute-start(bf16[512,512]{1,0:T(8,128)(2,1)} %bitcast.10), channel_id=1, source_target_pairs={{2,0},{3,1},{4,2},{5,3},{6,4},{7,5},{9,8},{11,10},{13,12},{15,14},... | collective-permute-start | bytes 1572872 | tf_op jit(solution)/shard_map/ppermute | solution.py:277
  20.7 21.9 %collective-permute-start.1 = (bf16[520,384]{1,0:T(8,128)(2,1)S(1)}, bf16[520,384]{1,0:T(8,128)(2,1)S(1)}, u32[]{:S(2)}, u32[]{:S(2)}) collective-permute-start(bf16[520,384]{1,0:T(8,128)(2,1)S(1)} %get-tuple-element.21), channel_id=1, source_target_pairs={{2,0},{3,1},{4,2},{5,3},{6,4},{7,5},{9,8},{11,10},{13,12},{15,14},... | collective-permute-start | bytes 1198088 | tf_op jit(solution)/shard_map/ppermute | solution.py:277
  23.3 20.8 %collective-permute-start.7 = (bf16[512,384]{1,0:T(8,128)(2,1)S(1)}, bf16[512,384]{1,0:T(8,128)(2,1)S(1)}, u32[]{:S(2)}, u32[]{:S(2)}) collective-permute-start(bf16[512,384]{1,0:T(8,128)(2,1)S(1)} %get-tuple-element.27), channel_id=1, source_target_pairs={{2,0},{3,1},{4,2},{5,3},{6,4},{7,5},{9,8},{11,10},{13,12},{15,14},... | collective-permute-start | bytes 1179656 | tf_op jit(solution)/shard_map/ppermute | solution.py:277
  32.7 13.1 %collective-permute-start.2 = (bf16[512,256]{1,0:T(8,128)(2,1)S(1)}, bf16[512,256]{1,0:T(8,128)(2,1)S(1)}, u32[]{:S(2)}, u32[]{:S(2)}) collective-permute-start(bf16[512,256]{1,0:T(8,128)(2,1)S(1)} %get-tuple-element.22), channel_id=1, source_target_pairs={{2,0},{3,1},{4,2},{5,3},{6,4},{7,5},{9,8},{11,10},{13,12},{15,14},... | collective-permute-start | bytes 786440 | tf_op jit(solution)/shard_map/ppermute | solution.py:277
